TPU v7x, 32 devices: a whole 2x2x4 slice. The times are simulated.
32 devices in a mesh: dp: 16 (over z, y, core), seq: 2 (over x).
Axes of the slice: x: 2, y: 2, z: 4, core: 2. Of those that a mesh axis runs over, the one named last changes fastest.
Arguments:
- inputs: bfloat16 [2, 2048, 1024], P(None, ('dp', 'seq')), may hold values from -6 to 6
- cotangent: bfloat16 [2, 2048, 1024], P(None, ('dp', 'seq')), may hold values from -6 to 6
- w_qkv: bfloat16 [1024, 3072], P('dp'), may hold values from -0.1875 to 0.1875
- w_out: bfloat16 [1024, 1024], P('dp'), may hold values from -0.75 to 0.75
- w_up: bfloat16 [1024, 4096], P('dp'), may hold values from -0.1875 to 0.1875
- w_down: bfloat16 [4096, 1024], P('dp'), may hold values from -0.09375 to 0.09375
- bias_q: bfloat16 [1024], P('dp'), may hold values from -3 to 3
- bias_v: bfloat16 [1024], P('dp'), may hold values from -3 to 3
- bias_out: bfloat16 [1024], P('dp'), may hold values from -3 to 3
- gain_one: bfloat16 [1024], P('dp'), may hold values from 0.5 to 1.5
- shift_one: bfloat16 [1024], P('dp'), may hold values from -3 to 3
- bias_up: bfloat16 [4096], P('dp'), may hold values from -3 to 3
- bias_down: bfloat16 [1024], P('dp'), may hold values from -3 to 3
- gain_two: bfloat16 [1024], P('dp'), may hold values from 0.5 to 1.5
- shift_two: bfloat16 [1024], P('dp'), may hold values from -3 to 3
Outputs:
- layer_out: bfloat16 [2, 2048, 1024], P(None, ('dp', 'seq'))
- input_grad: float32 [2, 2048, 1024], P(None, ('dp', 'seq'))
- grad_qkv: float32 [1024, 3072], P('dp')
- grad_out: float32 [1024, 1024], P('dp')
- grad_up: float32 [1024, 4096], P('dp')
- grad_down: float32 [4096, 1024], P('dp')
- grad_bias_q: float32 [1024], P('dp')
- grad_bias_v: float32 [1024], P('dp')
- grad_bias_out: float32 [1024], P('dp')
- grad_gain_one: float32 [1024], P('dp')
- grad_shift_one: float32 [1024], P('dp')
- grad_bias_up: float32 [4096], P('dp')
- grad_bias_down: float32 [1024], P('dp')
- grad_gain_two: float32 [1024], P('dp')
- grad_shift_two: float32 [1024], P('dp')
All inputs are finite; a program needn't handle non-finite values.
Results may differ from a plain program's by a relative error of at most 0.015.
Values may be sent and summed in bfloat16 or wider, within the bound.
No kernel may reach another device: no remote copies, remote signals or barrier semaphores. Data moves between devices by JAX's collectives and lax.ppermute only.
A program may use at most 192 MiB of HBM per device.

v0:
```python
import math
import jax
import jax.numpy as jnp
from jax import lax
from jax.sharding import PartitionSpec as P

HEAD = 64


def for_sending(shard):

    def short(part):
        return part.astype(jnp.bfloat16) if part.dtype == jnp.float32 else part

    return jax.tree.map(short, shard)


def normalize(features, gain, shift):
    centre = jnp.mean(features, axis=-1, keepdims=True)
    centred = features - centre
    spread = jnp.mean(centred * centred, axis=-1, keepdims=True)
    return centred * lax.rsqrt(spread + 1e-12) * gain + shift


def gelu_exact(values):
    return 0.5 * values * (1.0 + jax.scipy.special.erf(values * (1.0 / math.sqrt(2.0))))


def times_back(left, right):
    return lax.dot_general(
        left, right, (((1,), (1,)), ((), ())), preferred_element_type=jnp.float32
    )


def inner_rows(left, right):
    return lax.dot_general(
        left, right, (((0,), (0,)), ((), ())), preferred_element_type=jnp.float32
    )


def add_up(first_term, second_term):
    return first_term + second_term


def per_device(
    inputs,
    cotangent,
    w_qkv,
    w_out,
    w_up,
    w_down,
    bias_q,
    bias_v,
    bias_out,
    gain_one,
    shift_one,
    bias_up,
    bias_down,
    gain_two,
    shift_two,
):
    shards = (
        w_qkv,
        w_out,
        w_up,
        w_down,
        bias_q,
        bias_v,
        bias_out,
        gain_one,
        shift_one,
        bias_up,
        bias_down,
        gain_two,
        shift_two,
    )
    width = w_qkv.shape[1] // 3
    heads = width // HEAD
    scale = 1.0 / math.sqrt(HEAD)
    micro = inputs.shape[0]
    kept = []
    vector_total = None
    outputs = []
    input_grads = []
    for index in range(micro):
        full = (
            lax.all_gather(shards[0], "dp", axis=0, tiled=True),
            lax.all_gather(shards[1], "dp", axis=0, tiled=True),
            lax.all_gather(shards[2], "dp", axis=0, tiled=True),
            lax.all_gather(shards[3], "dp", axis=0, tiled=True),
            lax.all_gather(shards[4], "dp", axis=0, tiled=True),
            lax.all_gather(shards[5], "dp", axis=0, tiled=True),
            lax.all_gather(shards[6], "dp", axis=0, tiled=True),
            lax.all_gather(shards[7], "dp", axis=0, tiled=True),
            lax.all_gather(shards[8], "dp", axis=0, tiled=True),
            lax.all_gather(shards[9], "dp", axis=0, tiled=True),
            lax.all_gather(shards[10], "dp", axis=0, tiled=True),
            lax.all_gather(shards[11], "dp", axis=0, tiled=True),
            lax.all_gather(shards[12], "dp", axis=0, tiled=True),
        )
        full_qkv, full_out, full_up, full_down = (full[0], full[1], full[2], full[3])
        (
            query_bias,
            value_bias,
            out_bias,
            first_gain,
            first_shift,
            up_bias,
            down_bias,
            second_gain,
            second_shift,
        ) = [item.astype(jnp.float32) for item in full[4:]]
        tokens = inputs[index]
        rows = tokens.shape[0]
        qkv = jnp.dot(tokens, full_qkv, preferred_element_type=jnp.float32)
        queries = (qkv[:, :width] + query_bias).astype(jnp.bfloat16)
        keys = qkv[:, width : 2 * width].astype(jnp.bfloat16)
        values = (qkv[:, 2 * width :] + value_bias).astype(jnp.bfloat16)
        all_keys, all_values = (
            lax.all_gather(keys, "seq", axis=0, tiled=True),
            lax.all_gather(values, "seq", axis=0, tiled=True),
        )
        length = all_keys.shape[0]
        query_heads = queries.reshape(rows, heads, HEAD)
        key_heads = all_keys.reshape(length, heads, HEAD)
        value_heads = all_values.reshape(length, heads, HEAD)
        scores = (
            jnp.einsum("qhd,khd->hqk", query_heads, key_heads, preferred_element_type=jnp.float32)
            * scale
        )
        top = jnp.max(scores, axis=-1, keepdims=True)
        log_norm = top + jnp.log(jnp.sum(jnp.exp(scores - top), axis=-1, keepdims=True))
        probs = jnp.exp(scores - log_norm)
        probs_low = probs.astype(jnp.bfloat16)
        context = (
            jnp.einsum("hqk,khd->qhd", probs_low, value_heads, preferred_element_type=jnp.float32)
            .reshape(rows, width)
            .astype(jnp.bfloat16)
        )
        attended = jnp.dot(context, full_out, preferred_element_type=jnp.float32) + out_bias
        resid_one = tokens.astype(jnp.float32) + attended
        first = normalize(resid_one, first_gain, first_shift)
        first_low = first.astype(jnp.bfloat16)
        pre_act = jnp.dot(first_low, full_up, preferred_element_type=jnp.float32) + up_bias
        act = gelu_exact(pre_act).astype(jnp.bfloat16)
        mlp = jnp.dot(act, full_down, preferred_element_type=jnp.float32) + down_bias
        resid_two = first + mlp
        second = normalize(resid_two, second_gain, second_shift)
        outputs.append(second.astype(jnp.bfloat16))
        again = (
            lax.all_gather(w_qkv, "dp", axis=0, tiled=True),
            lax.all_gather(w_out, "dp", axis=0, tiled=True),
            lax.all_gather(w_up, "dp", axis=0, tiled=True),
            lax.all_gather(w_down, "dp", axis=0, tiled=True),
        )
        full_qkv, full_out, full_up, full_down = (again[0], again[1], again[2], again[3])
        incoming = cotangent[index].astype(jnp.float32)
        _, pull_two = jax.vjp(normalize, resid_two, second_gain, second_shift)
        grad_resid_two, grad_gain_b, grad_shift_b = pull_two(incoming)
        grad_mlp = grad_resid_two.astype(jnp.bfloat16)
        grad_act = times_back(grad_mlp, full_down)
        _, pull_gelu = jax.vjp(gelu_exact, pre_act)
        grad_pre = pull_gelu(grad_act)[0].astype(jnp.bfloat16)
        grad_first = grad_resid_two + times_back(grad_pre, full_up)
        _, pull_one = jax.vjp(normalize, resid_one, first_gain, first_shift)
        grad_resid_one, grad_gain_a, grad_shift_a = pull_one(grad_first)
        grad_attended = grad_resid_one.astype(jnp.bfloat16)
        grad_context = times_back(grad_attended, full_out).astype(jnp.bfloat16)
        grad_ctx_heads = grad_context.reshape(rows, heads, HEAD)
        grad_probs = jnp.einsum(
            "qhd,khd->hqk", grad_ctx_heads, value_heads, preferred_element_type=jnp.float32
        )
        grad_scores = (
            probs * (grad_probs - jnp.sum(probs * grad_probs, axis=-1, keepdims=True))
        ).astype(jnp.bfloat16)
        grad_queries = (
            (
                jnp.einsum(
                    "hqk,khd->qhd", grad_scores, key_heads, preferred_element_type=jnp.float32
                )
                * scale
            )
            .reshape(rows, width)
            .astype(jnp.bfloat16)
        )
        key_part = (
            jnp.einsum(
                "hqk,qhd->khd", grad_scores, query_heads, preferred_element_type=jnp.float32
            ).reshape(length, width)
            * scale
        )
        value_part = jnp.einsum(
            "hqk,qhd->khd", probs_low, grad_ctx_heads, preferred_element_type=jnp.float32
        ).reshape(length, width)
        grad_keys, grad_values = (
            lax.psum_scatter(
                key_part.astype(jnp.bfloat16), "seq", scatter_dimension=0, tiled=True
            ).astype(jnp.float32),
            lax.psum_scatter(
                value_part.astype(jnp.bfloat16), "seq", scatter_dimension=0, tiled=True
            ).astype(jnp.float32),
        )
        grad_values = grad_values.astype(jnp.bfloat16)
        grad_tokens = jnp.concatenate(
            [grad_queries, grad_keys.astype(jnp.bfloat16), grad_values], axis=1
        )
        input_grads.append(grad_resid_one + times_back(grad_tokens, full_qkv))
        vector_part = (
            jnp.sum(grad_queries.astype(jnp.float32), axis=0),
            jnp.sum(grad_values.astype(jnp.float32), axis=0),
            jnp.sum(grad_attended.astype(jnp.float32), axis=0),
            grad_gain_a,
            grad_shift_a,
            jnp.sum(grad_pre.astype(jnp.float32), axis=0),
            jnp.sum(grad_mlp.astype(jnp.float32), axis=0),
            grad_gain_b,
            grad_shift_b,
        )
        if vector_total is None:
            vector_total = vector_part
        else:
            vector_total = jax.tree.map(add_up, vector_total, vector_part)
        kept.append(
            (tokens, grad_tokens, context, grad_attended, first_low, grad_pre, act, grad_mlp)
        )
    stacked = [jnp.concatenate([entry[slot] for entry in kept], axis=0) for slot in range(8)]
    totals = (
        inner_rows(stacked[0], stacked[1]),
        inner_rows(stacked[2], stacked[3]),
        inner_rows(stacked[4], stacked[5]),
        inner_rows(stacked[6], stacked[7]),
    ) + tuple(vector_total)
    shares = lax.psum_scatter(totals, "dp", scatter_dimension=0, tiled=True)
    final = jax.tree.map(
        lambda part: part.astype(jnp.float32), lax.psum(for_sending(shares), "seq")
    )
    return (
        jnp.stack(outputs),
        jnp.stack(input_grads),
        final[0],
        final[1],
        final[2],
        final[3],
        final[4],
        final[5],
        final[6],
        final[7],
        final[8],
        final[9],
        final[10],
        final[11],
        final[12],
    )


def solution(mesh):
    placed = (
        P(None, ("dp", "seq"), None),
        P(None, ("dp", "seq"), None),
        P("dp", None),
        P("dp", None),
        P("dp", None),
        P("dp", None),
        P("dp"),
        P("dp"),
        P("dp"),
        P("dp"),
        P("dp"),
        P("dp"),
        P("dp"),
        P("dp"),
        P("dp"),
    )
    return jax.shard_map(
        per_device,
        mesh=mesh,
        in_specs=placed,
        out_specs=(
            P(None, ("dp", "seq"), None),
            P(None, ("dp", "seq"), None),
            P("dp", None),
            P("dp", None),
            P("dp", None),
            P("dp", None),
            P("dp"),
            P("dp"),
            P("dp"),
            P("dp"),
            P("dp"),
            P("dp"),
            P("dp"),
            P("dp"),
            P("dp"),
        ),
        check_vma=False,
    )
```

profile of v0, /device:TPU:0, one launch (start us, length us, event | category | flops | bytes accessed | tf_op | source)
XLA Modules:
  0.0 1044.0 jit_solution(4009803265087155789)
XLA Ops:
  18.7 64.1 %all-reduce.18 = (bf16[1024]{0:T(1024)(128)(2,1)S(1)}, bf16[1024]{0:T(1024)(128)(2,1)S(1)}, bf16[1024]{0:T(1024)(128)(2,1)S(1)}, bf16[1024]{0:T(1024)(128)(2,1)S...) all-reduce(bf16[1024]{0:T(1024)(128)(2,1)S(1)} %dynamic-update-slic, ...), channel_id=1, replica_groups=mesh['dp'=16,'seq'=2] {'dp'}, use_global_device_ids=true, to_apply=%add | all-reduce | flops 8192 | bytes 32768
  84.6 17.2 %all-gather = bf16[16,1,256]{2,1,0:T(2,128)(2,1)S(1)} all-gather(bf16[1,1,256]{2,1,0:T(2,128)(2,1)S(1)} %reshape.260), channel_id=1, replica_groups=mesh['dp'=16,'seq'=2] {'dp'}, dimensions={0}, use_global_device_ids=true | all-gather | bytes 8704 | tf_op jit(solution)/shard_map/all_gather | solution.py:96
  104.2 4.2 fusion.73
  110.4 6.4 all_gather.88
  117.0 5.7 all_gather.87
  123.1 5.6 all_gather.76
  128.9 6.2 all_gather.36
  137.8 2.3 fusion.82
  140.0 2.2 fusion.80
  143.7 50.2 %all-gather.10.cloned.1.call-done = bf16[1024,4096]{1,0:T(8,128)(2,1)} async-done(((bf16[64,4096]{1,0:T(8,128)(2,1)}), bf16[1024,4096]{1,0:T(8,128)(2,1)}) %all-gather.10.cloned.1.call-update) | async-done | bytes 8388624 | tf_op jit(solution)/shard_map/all_gather | solution.py:89
  193.9 6.0 multiply_convert_fusion
  199.9 69.2 %all-gather.12.cloned.1.call-done = bf16[4096,1024]{1,0:T(8,128)(2,1)} async-done(((bf16[256,1024]{1,0:T(8,128)(2,1)}), bf16[4096,1024]{1,0:T(8,128)(2,1)}) %all-gather.12.cloned.1.call-update) | async-done | bytes 8388624 | tf_op jit(solution)/shard_map/all_gather | solution.py:90
  269.1 5.2 fusion.84
  274.9 1.6 multiply_convert_fusion.1
  276.6 1.9 copy-done
  278.5 1.7 fusion.83
  283.9 3.5 convert_reduce_fusion
  287.3 2.8 convolution_add_fusion.6
  290.2 3.4 convert_reduce_fusion.1
  293.8 3.4 multiply_reduce_fusion.3
  302.2 1.7 copy.84
  304.0 2.0 convolution_convert_fusion.1
  308.5 1.9 fusion.1
  310.4 1.8 copy.73
  313.0 1.8 copy.75
  323.4 2.7 fusion.43
  328.8 7.4 reduce-scatter.11.cloned.1.call-done
  337.1 13.6 %reduce-scatter.13.cloned.1.call-done = bf16[64,1024]{1,0:T(8,128)(2,1)} async-done(((bf16[128,1024]{1,0:T(8,128)(2,1)}), bf16[64,1024]{1,0:T(8,128)(2,1)}) %reduce-scatter.13.cloned.1.call-update) | async-done | bytes 131088 | tf_op jit(solution)/shard_map/reduce_scatter | solution.py:196
  351.6 13.7 %reduce-scatter.15.cloned.1.call-done = bf16[64,1024]{1,0:T(8,128)(2,1)} async-done(((bf16[128,1024]{1,0:T(8,128)(2,1)}), bf16[64,1024]{1,0:T(8,128)(2,1)}) %reduce-scatter.15.cloned.1.call-update) | async-done | bytes 131088 | tf_op jit(solution)/shard_map/reduce_scatter | solution.py:199
  366.2 6.3 fusion.18
  373.7 8.9 fusion.14
  383.9 8.3 fusion.10
  392.5 49.1 %reduce-scatter.19.cloned.1.call-done = f32[64,1024]{1,0:T(8,128)} async-done(((f32[1024,1024]{1,0:T(8,128)}), f32[64,1024]{1,0:T(8,128)}) %reduce-scatter.19.cloned.1.call-update) | async-done | bytes 262160 | tf_op jit(solution)/shard_map/reduce_scatter | solution.py:233
  441.6 1.6 convert_element_type.381
  443.2 136.5 %reduce-scatter.17.cloned.1.call-done = f32[64,3072]{1,0:T(8,128)} async-done(((f32[1024,3072]{1,0:T(8,128)}), f32[64,3072]{1,0:T(8,128)}) %reduce-scatter.17.cloned.1.call-update) | async-done | bytes 786448 | tf_op jit(solution)/shard_map/reduce_scatter | solution.py:233
  579.7 1.9 convert_element_type.379
  581.6 180.5 %reduce-scatter.23.cloned.1.call-done = f32[256,1024]{1,0:T(8,128)} async-done(((f32[4096,1024]{1,0:T(8,128)}), f32[256,1024]{1,0:T(8,128)}) %reduce-scatter.23.cloned.1.call-update) | async-done | bytes 1048592 | tf_op jit(solution)/shard_map/reduce_scatter | solution.py:233
  762.1 2.1 convert_element_type.385
  764.2 180.0 %reduce-scatter.21.cloned.1.call-done = f32[64,4096]{1,0:T(8,128)} async-done(((f32[1024,4096]{1,0:T(8,128)}), f32[64,4096]{1,0:T(8,128)}) %reduce-scatter.21.cloned.1.call-update) | async-done | bytes 1048592 | tf_op jit(solution)/shard_map/reduce_scatter | solution.py:233
  944.2 2.1 convert_element_type.383
  948.7 59.7 %all-reduce.17 = (bf16[1024]{0:T(1024)(128)(2,1)S(1)}, bf16[1024]{0:T(1024)(128)(2,1)S(1)}, bf16[1024]{0:T(1024)(128)(2,1)S(1)}, bf16[1024]{0:T(1024)(128)(2,1)S...) all-reduce(f32[1024]{0:T(1024)S(1)} %add.318, ...), channel_id=10, replica_groups=mesh['dp'=16,'seq'=2] {'dp'}, use_global_device_ids=true, to_apply=%region_36.0.clone | all-reduce | flops 12288 | bytes 73728
  1009.1 5.2 all-reduce.19
  1019.0 4.8 fusion.5
  1023.8 4.8 fusion.4
  1029.4 2.1 convert_element_type.384
  1031.5 2.1 convert_element_type.386
  1033.6 1.9 convert_element_type.380
  1035.6 1.6 convert_element_type.382
  (322 shorter events, 57.5 us)
Async XLA Ops:
  7.2 101.3 %copy-start.15 = (bf16[2,64,1024]{2,1,0:T(8,128)(2,1)S(1)}, bf16[2,64,1024]{2,1,0:T(8,128)(2,1)}, u32[]{:S(2)}) copy-start(bf16[2,64,1024]{2,1,0:T(8,128)(2,1)} %param.15) | copy-start | bytes 786436
  7.2 97.0 %all-gather.6.cloned.1.call-start = ((), (), s32[]{:S(2)}) async-start(), calls=%async_computation.8 | async-start | bytes 6684672 | tf_op jit(solution)/shard_map/all_gather | solution.py:87
  7.9 129.8 %all-gather.8.cloned.1.call-start = ((), (), s32[]{:S(2)}) async-start(), calls=%async_computation.9 | async-start | bytes 2228224 | tf_op jit(solution)/shard_map/all_gather | solution.py:88
  8.7 185.2 %all-gather.10.cloned.1.call-start = ((), (), s32[]{:S(2)}) async-start(), calls=%async_computation.10 | async-start | bytes 8912896 | tf_op jit(solution)/shard_map/all_gather | solution.py:89
  9.4 259.7 %all-gather.12.cloned.1.call-start = ((), (), s32[]{:S(2)}) async-start(), calls=%async_computation.11 | async-start | bytes 8912896 | tf_op jit(solution)/shard_map/all_gather | solution.py:90
  10.0 317.9 %reduce-scatter.9.cloned.1.call-start = ((), (), s32[]{:S(2)}) async-start(), calls=%async_computation.12 | async-start | bytes 393216 | tf_op jit(solution)/shard_map/reduce_scatter | solution.py:196
  110.4 158.7 %copy-start.30 = (bf16[64,1024]{0,1:T(8,128)(2,1)}, bf16[64,1024]{0,1:T(8,128)(2,1)S(1)}, u32[]{:S(2)}) copy-start(bf16[64,1024]{0,1:T(8,128)(2,1)S(1)} %copy.83) | copy-start | bytes 393220
  135.3 64.6 %copy-start.33 = (bf16[128,1024]{0,1:T(8,128)(2,1)}, bf16[128,1024]{0,1:T(8,128)(2,1)S(1)}, u32[]{:S(2)}) copy-start(bf16[128,1024]{0,1:T(8,128)(2,1)S(1)} %copy.64) | copy-start | bytes 786436
  135.3 58.6 %copy-start.50 = (f32[16,1,256]{2,1,0:T(1,128)S(1)}, f32[16,1,256]{2,1,0:T(1,128)}, u32[]{:S(2)}) copy-start(f32[16,1,256]{2,1,0:T(1,128)} %convert_element_type.415) | copy-start | bytes 49156
  137.7 56.2 %copy-start.22 = (bf16[16,64,64]{2,1,0:T(8,128)(2,1)}, bf16[16,64,64]{2,1,0:T(8,128)(2,1)S(1)}, u32[]{:S(2)}) copy-start(bf16[16,64,64]{2,1,0:T(8,128)(2,1)S(1)} %convolution_convert_fusion.3) | copy-start | bytes 393220
  142.3 134.3 %copy-start.4 = (f32[64,1024]{1,0:T(8,128)}, f32[64,1024]{1,0:T(8,128)S(1)}, u32[]{:S(2)}) copy-start(f32[64,1024]{1,0:T(8,128)S(1)} %get-tuple-element.104) | copy-start | bytes 786436
  142.3 126.8 %copy-start.58 = (f32[64]{0:T(128)}, f32[64]{0:T(128)S(1)}, u32[]{:S(2)}) copy-start(f32[64]{0:T(128)S(1)} %get-tuple-element.126) | copy-start | bytes 772
  142.3 134.2 %copy-start.60 = (f32[64]{0:T(128)}, f32[64]{0:T(128)S(1)}, u32[]{:S(2)}) copy-start(f32[64]{0:T(128)S(1)} %get-tuple-element.127) | copy-start | bytes 772
  142.5 51.4 %copy-start.78 = (f32[64]{0:T(128)}, f32[64]{0:T(128)S(1)}, u32[]{:S(2)}) copy-start(f32[64]{0:T(128)S(1)} %multiply_reduce_fusion.7) | copy-start | bytes 772
  142.7 51.2 %copy-start.80 = (f32[64]{0:T(128)}, f32[64]{0:T(128)S(1)}, u32[]{:S(2)}) copy-start(f32[64]{0:T(128)S(1)} %multiply_reduce_fusion.9) | copy-start | bytes 772
  142.8 126.3 %copy-start.72 = (f32[64]{0:T(128)}, f32[64]{0:T(128)S(1)}, u32[]{:S(2)}) copy-start(f32[64]{0:T(128)S(1)} %fusion.66) | copy-start | bytes 772
  142.8 133.8 %copy-start.74 = (f32[64]{0:T(128)}, f32[64]{0:T(128)S(1)}, u32[]{:S(2)}) copy-start(f32[64]{0:T(128)S(1)} %fusion.64) | copy-start | bytes 772
  143.6 56.3 %copy-start.36 = (bf16[64,1024]{1,0:T(8,128)(2,1)}, bf16[64,1024]{1,0:T(8,128)(2,1)S(1)}, u32[]{:S(2)}) copy-start(bf16[64,1024]{1,0:T(8,128)(2,1)S(1)} %get-tuple-element.93) | copy-start | bytes 393220
  193.9 75.2 %copy-start.51 = (f32[1024]{0:T(1024)S(1)}, f32[1024]{0:T(1024)}, u32[]{:S(2)}) copy-start(f32[1024]{0:T(1024)} %convert_element_type.328) | copy-start | bytes 12292
  193.9 75.2 %copy-start.55 = (f32[1024]{0:T(1024)S(1)}, f32[1024]{0:T(1024)}, u32[]{:S(2)}) copy-start(f32[1024]{0:T(1024)} %convert_element_type.329) | copy-start | bytes 12292
  193.9 75.2 %copy-start.57 = (f32[1024]{0:T(1024)S(1)}, f32[1024]{0:T(1024)}, u32[]{:S(2)}) copy-start(f32[1024]{0:T(1024)} %convert_element_type.333) | copy-start | bytes 12292
  199.9 74.4 %copy-start.6 = (bf16[64,4096]{1,0:T(8,128)(2,1)}, bf16[64,4096]{1,0:T(8,128)(2,1)S(1)}, u32[]{:S(2)}) copy-start(bf16[64,4096]{1,0:T(8,128)(2,1)S(1)} %get-tuple-element.113) | copy-start | bytes 1572868
  312.3 23.9 %reduce-scatter.11.cloned.1.call-start = ((), (), s32[]{:S(2)}) async-start(), calls=%async_computation.13 | async-start | bytes 393216 | tf_op jit(solution)/shard_map/reduce_scatter | solution.py:199
  318.1 32.6 %reduce-scatter.13.cloned.1.call-start = ((), (), s32[]{:S(2)}) async-start(), calls=%async_computation.14 | async-start | bytes 393216 | tf_op jit(solution)/shard_map/reduce_scatter | solution.py:196
  322.0 43.3 %reduce-scatter.15.cloned.1.call-start = ((), (), s32[]{:S(2)}) async-start(), calls=%async_computation.15 | async-start | bytes 393216 | tf_op jit(solution)/shard_map/reduce_scatter | solution.py:199
  323.3 118.3 %reduce-scatter.19.cloned.1.call-start = ((), (), s32[]{:S(2)}) async-start(), calls=%async_computation.17 | async-start | bytes 4456448 | tf_op jit(solution)/shard_map/reduce_scatter | solution.py:233
  326.1 253.5 %reduce-scatter.17.cloned.1.call-start = ((), (), s32[]{:S(2)}) async-start(), calls=%async_computation.16 | async-start | bytes 13369344 | tf_op jit(solution)/shard_map/reduce_scatter | solution.py:233
  372.5 389.5 %reduce-scatter.23.cloned.1.call-start = ((), (), s32[]{:S(2)}) async-start(), calls=%async_computation.19 | async-start | bytes 17825792 | tf_op jit(solution)/shard_map/reduce_scatter | solution.py:233
  382.7 561.5 %reduce-scatter.21.cloned.1.call-start = ((), (), s32[]{:S(2)}) async-start(), calls=%async_computation.18 | async-start | bytes 17825792 | tf_op jit(solution)/shard_map/reduce_scatter | solution.py:233
  392.3 555.3 %copy-start.35 = (bf16[2,64,1024]{2,1,0:T(8,128)(2,1)S(1)}, bf16[2,64,1024]{2,1,0:T(8,128)(2,1)}, u32[]{:S(2)}) copy-start(bf16[2,64,1024]{2,1,0:T(8,128)(2,1)} %param.16) | copy-start | bytes 786436
  392.3 555.4 %copy-start.70 = (f32[1024]{0:T(1024)S(1)}, f32[1024]{0:T(1024)}, u32[]{:S(2)}) copy-start(f32[1024]{0:T(1024)} %get-tuple-element.69) | copy-start | bytes 12292
  392.3 555.4 %copy-start.68 = (f32[1024]{0:T(1024)S(1)}, f32[1024]{0:T(1024)}, u32[]{:S(2)}) copy-start(f32[1024]{0:T(1024)} %get-tuple-element.21) | copy-start | bytes 12292
  392.3 555.4 %copy-start.69 = (f32[1024]{0:T(1024)S(1)}, f32[1024]{0:T(1024)}, u32[]{:S(2)}) copy-start(f32[1024]{0:T(1024)} %get-tuple-element.98) | copy-start | bytes 12292
  392.3 555.4 %copy-start.66 = (f32[1024]{0:T(1024)S(1)}, f32[1024]{0:T(1024)}, u32[]{:S(2)}) copy-start(f32[1024]{0:T(1024)} %get-tuple-element.28) | copy-start | bytes 12292
  392.3 555.4 %copy-start.67 = (f32[1024]{0:T(1024)S(1)}, f32[1024]{0:T(1024)}, u32[]{:S(2)}) copy-start(f32[1024]{0:T(1024)} %get-tuple-element.96) | copy-start | bytes 12292
  392.4 555.4 %copy-start.53 = (f32[4096]{0:T(1024)S(1)}, f32[4096]{0:T(1024)}, u32[]{:S(2)}) copy-start(f32[4096]{0:T(1024)} %get-tuple-element.63) | copy-start | bytes 49156
  392.4 555.4 %copy-start.54 = (f32[4096]{0:T(1024)S(1)}, f32[4096]{0:T(1024)}, u32[]{:S(2)}) copy-start(f32[4096]{0:T(1024)} %get-tuple-element.65) | copy-start | bytes 49156
  392.4 555.4 %copy-start.64 = (f32[1024]{0:T(1024)S(1)}, f32[1024]{0:T(1024)}, u32[]{:S(2)}) copy-start(f32[1024]{0:T(1024)} %get-tuple-element.61) | copy-start | bytes 12292
  392.4 555.4 %copy-start.65 = (f32[1024]{0:T(1024)S(1)}, f32[1024]{0:T(1024)}, u32[]{:S(2)}) copy-start(f32[1024]{0:T(1024)} %get-tuple-element.59) | copy-start | bytes 12292
  392.4 555.4 %copy-start.62 = (f32[1024]{0:T(1024)S(1)}, f32[1024]{0:T(1024)}, u32[]{:S(2)}) copy-start(f32[1024]{0:T(1024)} %get-tuple-element.17) | copy-start | bytes 12292
  392.4 555.4 %copy-start.63 = (f32[1024]{0:T(1024)S(1)}, f32[1024]{0:T(1024)}, u32[]{:S(2)}) copy-start(f32[1024]{0:T(1024)} %get-tuple-element.24) | copy-start | bytes 12292
  392.4 555.5 %copy-start.46 = (bf16[1,64,1024]{2,1,0:T(8,128)(2,1)S(1)}, bf16[1,64,1024]{2,1,0:T(8,128)(2,1)}, u32[]{:S(2)}) copy-start(bf16[1,64,1024]{2,1,0:T(8,128)(2,1)} %get-tuple-element.84) | copy-start | bytes 393220
  392.4 555.5 %copy-start.47 = (bf16[1,64,1024]{2,1,0:T(8,128)(2,1)S(1)}, bf16[1,64,1024]{2,1,0:T(8,128)(2,1)}, u32[]{:S(2)}) copy-start(bf16[1,64,1024]{2,1,0:T(8,128)(2,1)} %get-tuple-element.85) | copy-start | bytes 393220
  392.4 556.2 %copy-start.48 = (bf16[64,1024]{1,0:T(8,128)(2,1)S(1)}, bf16[64,1024]{1,0:T(8,128)(2,1)}, u32[]{:S(2)}) copy-start(bf16[64,1024]{1,0:T(8,128)(2,1)} %reduce-scatter.11.cloned.1.call-done) | copy-start | bytes 393220
  392.4 556.2 %copy-start.49 = (bf16[64,1024]{1,0:T(8,128)(2,1)S(1)}, bf16[64,1024]{1,0:T(8,128)(2,1)}, u32[]{:S(2)}) copy-start(bf16[64,1024]{1,0:T(8,128)(2,1)} %reduce-scatter.15.cloned.1.call-done) | copy-start | bytes 393220
  392.5 626.5 %copy-start.19 = (f32[64,1024]{1,0:T(8,128)S(1)}, f32[64,1024]{1,0:T(8,128)}, u32[]{:S(2)}) copy-start(f32[64,1024]{1,0:T(8,128)} %copy-done.18) | copy-start | bytes 786436
  392.5 626.5 %copy-start.77 = (f32[64]{0:T(128)S(1)}, f32[64]{0:T(128)}, u32[]{:S(2)}) copy-start(f32[64]{0:T(128)} %copy-done.76) | copy-start | bytes 772
  392.5 637.0 %all-reduce.23.cloned.1.call-start = ((), (), s32[]{:S(2)}) async-start(), calls=%async_computation.20 | async-start | bytes 3145728 | tf_op jit(solution)/shard_map/psum | solution.py:235
  (47 other events, 249.6 us)
Sparse Core Ops, SparseCore 0:
  10.3 65.4 all-gather.5
  78.0 39.9 all-gather.7
  120.2 73.6 all-gather.9
  195.9 73.1 all-gather.11
  312.4 9.8 reduce-scatter.8
  324.5 11.6 reduce-scatter.10
  339.0 11.6 reduce-scatter.12
  353.6 11.6 reduce-scatter.14
  369.1 72.4 reduce-scatter.18
  446.0 133.5 reduce-scatter.16
  584.3 177.6 reduce-scatter.22
  766.6 177.5 reduce-scatter.20
  947.3 51.0 all-reduce.22
where the time goes:
time: 1050 us; the launch traced here: 1040 us
  waiting for transfers between devices  703 us (67%)
  blocking collectives  170 us (16%)
  matrix products  86.8 us (8%)
  other arithmetic  35.1 us (3%)
  local copies, waits for them, and re-layouts  31 us (3%)
  between operations  17.5 us (2%)
    reduce_scatter x4, waiting for transfers between devices, per_device(): shares = lax.psum_scatter(totals, 'dp', scatter_dimension=0, tiled=True)  546 us
    unnamed x2, blocking collectives  124 us
    all_gather x1, waiting for transfers between devices, per_device(): lax.all_gather(shards[3], 'dp', axis=0, tiled=True)  69.2 us
    all_gather x1, waiting for transfers between devices, per_device(): lax.all_gather(shards[2], 'dp', axis=0, tiled=True)  50.2 us
    dot_general x4, matrix products, inner_rows(): lax.dot_general(left, right, (((0,), (0,)), ((), ())), preferred_element_...  26.3 us
    dot_general x8, matrix products, times_back(): lax.dot_general(left, right, (((1,), (1,)), ((), ())), preferred_element_...  25.6 us
    reduce_scatter x2, waiting for transfers between devices, per_device(): lax.psum_scatter(value_part.astype(jnp.bfloat16), 'seq', scatter_dimensio...  21.1 us
  transfers between devices with their start and end apart: 13, of which 9 were waited for; matrix products, arithmetic and copies ran while one was open for 9% of the time, Pallas kernels for 0%

commit v1 on v0

--- a/solution.py
+++ b/solution.py
@@ -5,6 +5,27 @@
 from jax.sharding import PartitionSpec as P
 
 HEAD = 64
+
+
+def ring_gather(x, axis, dim):
+    size, place, rows = (lax.axis_size(axis), lax.axis_index(axis), x.shape[dim])
+    right = [(i, (i + 1) % size) for i in range(size)]
+    backward = [(i, (i - 1) % size) for i in range(size)]
+    whole = jnp.zeros((*x.shape[:dim], size * rows, *x.shape[dim + 1 :]), x.dtype)
+    whole = lax.dynamic_update_slice_in_dim(whole, x, place * rows, axis=dim)
+    from_left = from_right = x
+    half = size // 2
+    for step in range(1, half + 1):
+        from_left = lax.ppermute(from_left, axis, right)
+        whole = lax.dynamic_update_slice_in_dim(
+            whole, from_left, (place - step) % size * rows, axis=dim
+        )
+        if step < size - half:
+            from_right = lax.ppermute(from_right, axis, backward)
+            whole = lax.dynamic_update_slice_in_dim(
+                whole, from_right, (place + step) % size * rows, axis=dim
+            )
+    return whole
 
 
 def for_sending(shard):
@@ -87,7 +108,7 @@
             lax.all_gather(shards[0], "dp", axis=0, tiled=True),
             lax.all_gather(shards[1], "dp", axis=0, tiled=True),
             lax.all_gather(shards[2], "dp", axis=0, tiled=True),
-            lax.all_gather(shards[3], "dp", axis=0, tiled=True),
+            ring_gather(shards[3], "dp", 0),
             lax.all_gather(shards[4], "dp", axis=0, tiled=True),
             lax.all_gather(shards[5], "dp", axis=0, tiled=True),
             lax.all_gather(shards[6], "dp", axis=0, tiled=True),

time: 1050 us -> 1090 us (1.038)
  starting transfers between devices: 0.74 us -> 42.6 us
  waiting for transfers between devices: 703 us -> 680 us
  local copies, waits for them, and re-layouts: 31 us -> 46.2 us
  matrix products: 86.8 us -> 98 us
    ppermute x0 -> x15, waiting for transfers between devices: none -> 67.9 us  [the longest x8 50.5 us: ring_gather(): from_left = lax.ppermute(from_left, axis, right)]
    all_gather x1, waiting for transfers between devices: 50.2 us -> 0.02 us  [per_device(): lax.all_gather(shards[2], 'dp', axis=0, tiled=True)]
    ppermute x0 -> x15, starting transfers between devices: none -> 41.9 us  [the longest x7 21.6 us: ring_gather(): from_right = lax.ppermute(from_right, axis, backward)]
    all_gather x1, waiting for transfers between devices: 69.2 us -> 29.4 us  [per_device(): lax.all_gather(w_down, 'dp', axis=0, tiled=True)]
    dynamic_update_slice x0 -> x16, local copies, waits for them, and re-layouts: none -> 19.7 us  [the longest x8 10.9 us: ring_gather(): lax.dynamic_update_slice_in_dim(whole, from_left, (place - step) % size *...]
  transfers between devices with their start and end apart: 13 -> 28, of which waited for: 9 -> 16; matrix products, arithmetic and copies ran while one was open for 9% -> 12% of each run, Pallas kernels for 0% -> 0%
where the time goes in v1:
time: 1090 us; the launch traced here: 1080 us
  waiting for transfers between devices  680 us (62%)
  blocking collectives  167 us (15%)
  matrix products  98 us (9%)
  local copies, waits for them, and re-layouts  46.2 us (4%)
  starting transfers between devices  42.6 us (4%)
  other arithmetic  30.9 us (3%)
  between operations  17.8 us (2%)
    reduce_scatter x4, waiting for transfers between devices, per_device(): shares = lax.psum_scatter(totals, 'dp', scatter_dimension=0, tiled=True)  546 us
    unnamed x2, blocking collectives  120 us
    ppermute x8, waiting for transfers between devices, ring_gather(): from_left = lax.ppermute(from_left, axis, right)  50.5 us
    dot_general x8, matrix products, times_back(): lax.dot_general(left, right, (((1,), (1,)), ((), ())), preferred_element_...  32.7 us
    all_gather x1, waiting for transfers between devices, per_device(): lax.all_gather(w_down, 'dp', axis=0, tiled=True)  29.4 us
    dot_general x4, matrix products, inner_rows(): lax.dot_general(left, right, (((0,), (0,)), ((), ())), preferred_element_...  27.3 us
  transfers between devices with their start and end apart: 28, of which 16 were waited for; matrix products, arithmetic and copies ran while one was open for 12% of the time, Pallas kernels for 0%

profile of v1, /device:TPU:0, one launch (start us, length us, event | category | flops | bytes accessed | tf_op | source)
XLA Modules:
  0.0 1082.2 jit_solution(1283007268162980714)
XLA Ops:
  10.6 5.1 collective-permute-start.1
  15.7 7.1 collective-permute-done
  22.8 6.7 collective-permute-start.2
  29.6 15.5 %collective-permute-done.2 = bf16[256,1024]{1,0:T(8,128)(2,1)S(1)} collective-permute-done((bf16[256,1024]{1,0:T(8,128)(2,1)S(1)}, bf16[256,1024]{1,0:T(8,128)(2,1)S(1)}, u32[]{:S(2)}, u32[]{:S(2)}) %collective-permute-start.2) | collective-permute-done | bytes 524320 | tf_op jit(solution)/shard_map/ppermute | solution.py:19
  45.1 4.4 collective-permute-start.5
  49.5 11.3 %collective-permute-done.4 = bf16[256,1024]{1,0:T(8,128)(2,1)S(1)} collective-permute-done((bf16[256,1024]{1,0:T(8,128)(2,1)S(1)}, bf16[256,1024]{1,0:T(8,128)(2,1)S(1)}, u32[]{:S(2)}, u32[]{:S(2)}) %collective-permute-start.4) | collective-permute-done | bytes 524320 | tf_op jit(solution)/shard_map/ppermute | solution.py:19
  60.8 6.5 collective-permute-done.5
  67.3 4.7 collective-permute-start.7
  71.9 5.2 collective-permute-done.6
  77.1 5.8 collective-permute-start.8
  83.6 7.4 collective-permute-done.8
  91.1 5.1 collective-permute-start.10
  96.1 4.3 broadcast.203
  104.5 60.6 %all-reduce.18 = (bf16[1024]{0:T(1024)(128)(2,1)S(1)}, bf16[1024]{0:T(1024)(128)(2,1)S(1)}, bf16[1024]{0:T(1024)(128)(2,1)S(1)}, bf16[1024]{0:T(1024)(128)(2,1)S...) all-reduce(bf16[1024]{0:T(1024)(128)(2,1)S(1)} %dynamic-update-slic, ...), channel_id=1, replica_groups=mesh['dp'=16,'seq'=2] {'dp'}, use_global_device_ids=true, to_apply=%add | all-reduce | flops 8192 | bytes 32768
  165.1 17.2 %all-gather = bf16[16,1,256]{2,1,0:T(2,128)(2,1)S(1)} all-gather(bf16[1,1,256]{2,1,0:T(2,128)(2,1)S(1)} %reshape.260), channel_id=1, replica_groups=mesh['dp'=16,'seq'=2] {'dp'}, dimensions={0}, use_global_device_ids=true | all-gather | bytes 8704 | tf_op jit(solution)/shard_map/all_gather | solution.py:117
  195.4 10.9 %collective-permute-done.11 = bf16[256,1024]{1,0:T(8,128)(2,1)S(1)} collective-permute-done((bf16[256,1024]{1,0:T(8,128)(2,1)S(1)}, bf16[256,1024]{1,0:T(8,128)(2,1)S(1)}, u32[]{:S(2)}, u32[]{:S(2)}) %collective-permute-start.11) | collective-permute-done | bytes 524320 | tf_op jit(solution)/shard_map/ppermute | solution.py:24
  206.3 4.7 collective-permute-start.13
  212.9 2.3 collective-permute-start.14
  220.4 4.0 collective-permute-done.14
  225.3 4.1 fusion.73
  231.4 5.6 all_gather.85
  237.2 5.6 all_gather.84
  243.2 5.6 all_gather.74
  249.1 7.3 all_gather.72
  264.5 5.2 multiply_convert_fusion
  269.8 5.3 fusion.84
  275.3 2.7 multiply_convert_fusion.1
  278.0 5.3 fusion.83
  287.1 29.4 %all-gather.12.cloned.1.call-done = bf16[4096,1024]{1,0:T(8,128)(2,1)} async-done(((bf16[256,1024]{1,0:T(8,128)(2,1)}), bf16[4096,1024]{1,0:T(8,128)(2,1)}) %all-gather.12.cloned.1.call-update) | async-done | bytes 8388624 | tf_op jit(solution)/shard_map/all_gather | solution.py:175
  316.5 7.0 convert_reduce_fusion
  323.5 6.4 convolution_add_fusion.6
  330.0 3.5 convert_reduce_fusion.1
  333.6 3.4 multiply_reduce_fusion.3
  361.5 3.8 fusion.43
  368.0 6.2 reduce-scatter.11.cloned.1.call-done
  375.2 13.6 %reduce-scatter.13.cloned.1.call-done = bf16[64,1024]{1,0:T(8,128)(2,1)} async-done(((bf16[128,1024]{1,0:T(8,128)(2,1)}), bf16[64,1024]{1,0:T(8,128)(2,1)}) %reduce-scatter.13.cloned.1.call-update) | async-done | bytes 131088 | tf_op jit(solution)/shard_map/reduce_scatter | solution.py:217
  389.6 13.7 %reduce-scatter.15.cloned.1.call-done = bf16[64,1024]{1,0:T(8,128)(2,1)} async-done(((bf16[128,1024]{1,0:T(8,128)(2,1)}), bf16[64,1024]{1,0:T(8,128)(2,1)}) %reduce-scatter.15.cloned.1.call-update) | async-done | bytes 131088 | tf_op jit(solution)/shard_map/reduce_scatter | solution.py:220
  404.2 6.3 fusion.18
  411.8 8.9 fusion.14
  421.9 8.4 fusion.10
  430.5 49.1 %reduce-scatter.19.cloned.1.call-done = f32[64,1024]{1,0:T(8,128)} async-done(((f32[1024,1024]{1,0:T(8,128)}), f32[64,1024]{1,0:T(8,128)}) %reduce-scatter.19.cloned.1.call-update) | async-done | bytes 262160 | tf_op jit(solution)/shard_map/reduce_scatter | solution.py:254
  481.3 136.5 %reduce-scatter.17.cloned.1.call-done = f32[64,3072]{1,0:T(8,128)} async-done(((f32[1024,3072]{1,0:T(8,128)}), f32[64,3072]{1,0:T(8,128)}) %reduce-scatter.17.cloned.1.call-update) | async-done | bytes 786448 | tf_op jit(solution)/shard_map/reduce_scatter | solution.py:254
  619.7 180.5 %reduce-scatter.23.cloned.1.call-done = f32[256,1024]{1,0:T(8,128)} async-done(((f32[4096,1024]{1,0:T(8,128)}), f32[256,1024]{1,0:T(8,128)}) %reduce-scatter.23.cloned.1.call-update) | async-done | bytes 1048592 | tf_op jit(solution)/shard_map/reduce_scatter | solution.py:254
  802.3 180.0 %reduce-scatter.21.cloned.1.call-done = f32[64,4096]{1,0:T(8,128)} async-done(((f32[1024,4096]{1,0:T(8,128)}), f32[64,4096]{1,0:T(8,128)}) %reduce-scatter.21.cloned.1.call-update) | async-done | bytes 1048592 | tf_op jit(solution)/shard_map/reduce_scatter | solution.py:254
  986.9 59.7 %all-reduce.17 = (bf16[1024]{0:T(1024)(128)(2,1)S(1)}, bf16[1024]{0:T(1024)(128)(2,1)S(1)}, bf16[1024]{0:T(1024)(128)(2,1)S(1)}, bf16[1024]{0:T(1024)(128)(2,1)S...) all-reduce(f32[1024]{0:T(1024)S(1)} %add.517, ...), channel_id=10, replica_groups=mesh['dp'=16,'seq'=2] {'dp'}, use_global_device_ids=true, to_apply=%region_36.37.clone | all-reduce | flops 12288 | bytes 73728
  1047.3 5.2 all-reduce.19
  1057.2 4.8 fusion.5
  1062.0 4.8 fusion.4
  (398 shorter events, 97.7 us)
Async XLA Ops:
  7.3 157.8 %copy-start.88 = (bf16[256]{0:T(256)(128)(2,1)S(1)}, bf16[256]{0:T(256)(128)(2,1)}, u32[]{:S(2)}) copy-start(bf16[256]{0:T(256)(128)(2,1)} %param.26) | copy-start | bytes 1540
  7.3 218.0 %all-gather.6.cloned.1.call-start = ((), (), s32[]{:S(2)}) async-start(), calls=%async_computation.8 | async-start | bytes 6684672 | tf_op jit(solution)/shard_map/all_gather | solution.py:108
  8.0 250.9 %all-gather.8.cloned.1.call-start = ((), (), s32[]{:S(2)}) async-start(), calls=%async_computation.9 | async-start | bytes 2228224 | tf_op jit(solution)/shard_map/all_gather | solution.py:109
  8.8 255.7 %all-gather.10.cloned.1.call-start = ((), (), s32[]{:S(2)}) async-start(), calls=%async_computation.10 | async-start | bytes 8912896 | tf_op jit(solution)/shard_map/all_gather | solution.py:110
  9.5 306.9 %all-gather.12.cloned.1.call-start = ((), (), s32[]{:S(2)}) async-start(), calls=%async_computation.11 | async-start | bytes 8912896 | tf_op jit(solution)/shard_map/all_gather | solution.py:175
  10.1 357.0 %reduce-scatter.9.cloned.1.call-start = ((), (), s32[]{:S(2)}) async-start(), calls=%async_computation.12 | async-start | bytes 393216 | tf_op jit(solution)/shard_map/reduce_scatter | solution.py:217
  10.1 12.7 %collective-permute-start = (bf16[256,1024]{1,0:T(8,128)(2,1)}, bf16[256,1024]{1,0:T(8,128)(2,1)S(1)}, u32[]{:S(2)}, u32[]{:S(2)}) collective-permute-start(bf16[256,1024]{1,0:T(8,128)(2,1)} %param.20), channel_id=1, source_target_pairs={{0,2},{2,4},{4,6},{6,8},{8,10},{10,12},{12,14},{14,16},{16,18},{18... | collective-permute-start | bytes 1572872 | tf_op jit(solution)/shard_map/ppermute | solution.py:19
  10.6 18.9 %collective-permute-start.1 = (bf16[256,1024]{1,0:T(8,128)(2,1)}, bf16[256,1024]{1,0:T(8,128)(2,1)S(1)}, u32[]{:S(2)}, u32[]{:S(2)}) collective-permute-start(bf16[256,1024]{1,0:T(8,128)(2,1)} %param.20), channel_id=1, source_target_pairs={{0,30},{2,0},{4,2},{6,4},{8,6},{10,8},{12,10},{14,12},{16,14},{18,... | collective-permute-start | bytes 1572872 | tf_op jit(solution)/shard_map/ppermute | solution.py:24
  22.8 22.2 %collective-permute-start.2 = (bf16[256,1024]{1,0:T(8,128)(2,1)S(1)}, bf16[256,1024]{1,0:T(8,128)(2,1)S(1)}, u32[]{:S(2)}, u32[]{:S(2)}) collective-permute-start(bf16[256,1024]{1,0:T(8,128)(2,1)S(1)} %collective-permute-done), channel_id=1, source_target_pairs={{0,2},{2,4},{4,6},{6,8},{8,10},{10,12},{12,14},{14,16},{16,18},{18... | collective-permute-start | bytes 1572872 | tf_op jit(solution)/shard_map/ppermute | solution.py:19
  29.6 15.5 %collective-permute-start.3 = (bf16[256,1024]{1,0:T(8,128)(2,1)S(1)}, bf16[256,1024]{1,0:T(8,128)(2,1)S(1)}, u32[]{:S(2)}, u32[]{:S(2)}) collective-permute-start(bf16[256,1024]{1,0:T(8,128)(2,1)S(1)} %collective-permute-done.1), channel_id=1, source_target_pairs={{0,30},{2,0},{4,2},{6,4},{8,6},{10,8},{12,10},{14,12},{16,14},{18,... | collective-permute-start | bytes 1572872 | tf_op jit(solution)/shard_map/ppermute | solution.py:24
  45.1 15.7 %collective-permute-start.4 = (bf16[256,1024]{1,0:T(8,128)(2,1)S(1)}, bf16[256,1024]{1,0:T(8,128)(2,1)S(1)}, u32[]{:S(2)}, u32[]{:S(2)}) collective-permute-start(bf16[256,1024]{1,0:T(8,128)(2,1)S(1)} %collective-permute-done.2), channel_id=1, source_target_pairs={{0,2},{2,4},{4,6},{6,8},{8,10},{10,12},{12,14},{14,16},{16,18},{18... | collective-permute-start | bytes 1572872 | tf_op jit(solution)/shard_map/ppermute | solution.py:19
  45.1 22.2 %collective-permute-start.5 = (bf16[256,1024]{1,0:T(8,128)(2,1)S(1)}, bf16[256,1024]{1,0:T(8,128)(2,1)S(1)}, u32[]{:S(2)}, u32[]{:S(2)}) collective-permute-start(bf16[256,1024]{1,0:T(8,128)(2,1)S(1)} %collective-permute-done.3), channel_id=1, source_target_pairs={{0,30},{2,0},{4,2},{6,4},{8,6},{10,8},{12,10},{14,12},{16,14},{18,... | collective-permute-start | bytes 1572872 | tf_op jit(solution)/shard_map/ppermute | solution.py:24
  60.8 16.4 %collective-permute-start.6 = (bf16[256,1024]{1,0:T(8,128)(2,1)S(1)}, bf16[256,1024]{1,0:T(8,128)(2,1)}, u32[]{:S(2)}, u32[]{:S(2)}) collective-permute-start(bf16[256,1024]{1,0:T(8,128)(2,1)S(1)} %collective-permute-done.4), channel_id=1, source_target_pairs={{0,2},{2,4},{4,6},{6,8},{8,10},{10,12},{12,14},{14,16},{16,18},{18... | collective-permute-start | bytes 1572872 | tf_op jit(solution)/shard_map/ppermute | solution.py:19
  67.3 15.7 %collective-permute-start.7 = (bf16[256,1024]{1,0:T(8,128)(2,1)S(1)}, bf16[256,1024]{1,0:T(8,128)(2,1)}, u32[]{:S(2)}, u32[]{:S(2)}) collective-permute-start(bf16[256,1024]{1,0:T(8,128)(2,1)S(1)} %collective-permute-done.5), channel_id=1, source_target_pairs={{0,30},{2,0},{4,2},{6,4},{8,6},{10,8},{12,10},{14,12},{16,14},{18,... | collective-permute-start | bytes 1572872 | tf_op jit(solution)/shard_map/ppermute | solution.py:24
  77.1 13.9 %collective-permute-start.8 = (bf16[256,1024]{1,0:T(8,128)(2,1)}, bf16[256,1024]{1,0:T(8,128)(2,1)}, u32[]{:S(2)}, u32[]{:S(2)}) collective-permute-start(bf16[256,1024]{1,0:T(8,128)(2,1)} %collective-permute-done.6), channel_id=1, source_target_pairs={{0,2},{2,4},{4,6},{6,8},{8,10},{10,12},{12,14},{14,16},{16,18},{18... | collective-permute-start | bytes 1572872 | tf_op jit(solution)/shard_map/ppermute | solution.py:19
  82.9 104.2 %collective-permute-start.9 = (bf16[256,1024]{1,0:T(8,128)(2,1)}, bf16[256,1024]{1,0:T(8,128)(2,1)S(1)}, u32[]{:S(2)}, u32[]{:S(2)}) collective-permute-start(bf16[256,1024]{1,0:T(8,128)(2,1)} %collective-permute-done.7), channel_id=1, source_target_pairs={{0,30},{2,0},{4,2},{6,4},{8,6},{10,8},{12,10},{14,12},{16,14},{18,... | collective-permute-start | bytes 1572872 | tf_op jit(solution)/shard_map/ppermute | solution.py:24
  91.1 98.9 %collective-permute-start.10 = (bf16[256,1024]{1,0:T(8,128)(2,1)}, bf16[256,1024]{1,0:T(8,128)(2,1)}, u32[]{:S(2)}, u32[]{:S(2)}) collective-permute-start(bf16[256,1024]{1,0:T(8,128)(2,1)} %collective-permute-done.8), channel_id=1, source_target_pairs={{0,2},{2,4},{4,6},{6,8},{8,10},{10,12},{12,14},{14,16},{16,18},{18... | collective-permute-start | bytes 1572872 | tf_op jit(solution)/shard_map/ppermute | solution.py:19
  101.3 123.9 %copy-start.13 = (bf16[2,64,1024]{2,1,0:T(8,128)(2,1)S(1)}, bf16[2,64,1024]{2,1,0:T(8,128)(2,1)}, u32[]{:S(2)}) copy-start(bf16[2,64,1024]{2,1,0:T(8,128)(2,1)} %param.15) | copy-start | bytes 786436
  187.2 19.2 %collective-permute-start.11 = (bf16[256,1024]{1,0:T(8,128)(2,1)S(1)}, bf16[256,1024]{1,0:T(8,128)(2,1)S(1)}, u32[]{:S(2)}, u32[]{:S(2)}) collective-permute-start(bf16[256,1024]{1,0:T(8,128)(2,1)S(1)} %collective-permute-done.9), channel_id=1, source_target_pairs={{0,30},{2,0},{4,2},{6,4},{8,6},{10,8},{12,10},{14,12},{16,14},{18,... | collective-permute-start | bytes 1572872 | tf_op jit(solution)/shard_map/ppermute | solution.py:24
  190.0 22.9 %collective-permute-start.12 = (bf16[256,1024]{1,0:T(8,128)(2,1)}, bf16[256,1024]{1,0:T(8,128)(2,1)S(1)}, u32[]{:S(2)}, u32[]{:S(2)}) collective-permute-start(bf16[256,1024]{1,0:T(8,128)(2,1)} %collective-permute-done.10), channel_id=1, source_target_pairs={{0,2},{2,4},{4,6},{6,8},{8,10},{10,12},{12,14},{14,16},{16,18},{18... | collective-permute-start | bytes 1572872 | tf_op jit(solution)/shard_map/ppermute | solution.py:19
  206.3 13.3 %collective-permute-start.13 = (bf16[256,1024]{1,0:T(8,128)(2,1)S(1)}, bf16[256,1024]{1,0:T(8,128)(2,1)S(1)}, u32[]{:S(2)}, u32[]{:S(2)}) collective-permute-start(bf16[256,1024]{1,0:T(8,128)(2,1)S(1)} %collective-permute-done.11), channel_id=1, source_target_pairs={{0,30},{2,0},{4,2},{6,4},{8,6},{10,8},{12,10},{14,12},{16,14},{18,... | collective-permute-start | bytes 1572872 | tf_op jit(solution)/shard_map/ppermute | solution.py:24
  212.9 11.5 %collective-permute-start.14 = (bf16[256,1024]{1,0:T(8,128)(2,1)S(1)}, bf16[256,1024]{1,0:T(8,128)(2,1)S(1)}, u32[]{:S(2)}, u32[]{:S(2)}) collective-permute-start(bf16[256,1024]{1,0:T(8,128)(2,1)S(1)} %collective-permute-done.12), channel_id=1, source_target_pairs={{0,2},{2,4},{4,6},{6,8},{8,10},{10,12},{12,14},{14,16},{16,18},{18... | collective-permute-start | bytes 1572872 | tf_op jit(solution)/shard_map/ppermute | solution.py:19
  350.4 23.8 %reduce-scatter.11.cloned.1.call-start = ((), (), s32[]{:S(2)}) async-start(), calls=%async_computation.13 | async-start | bytes 393216 | tf_op jit(solution)/shard_map/reduce_scatter | solution.py:220
  356.3 32.4 %reduce-scatter.13.cloned.1.call-start = ((), (), s32[]{:S(2)}) async-start(), calls=%async_computation.14 | async-start | bytes 393216 | tf_op jit(solution)/shard_map/reduce_scatter | solution.py:217
  360.2 43.1 %reduce-scatter.15.cloned.1.call-start = ((), (), s32[]{:S(2)}) async-start(), calls=%async_computation.15 | async-start | bytes 393216 | tf_op jit(solution)/shard_map/reduce_scatter | solution.py:220
  361.5 118.2 %reduce-scatter.19.cloned.1.call-start = ((), (), s32[]{:S(2)}) async-start(), calls=%async_computation.17 | async-start | bytes 4456448 | tf_op jit(solution)/shard_map/reduce_scatter | solution.py:254
  365.3 252.5 %reduce-scatter.17.cloned.1.call-start = ((), (), s32[]{:S(2)}) async-start(), calls=%async_computation.16 | async-start | bytes 13369344 | tf_op jit(solution)/shard_map/reduce_scatter | solution.py:254
  410.6 389.7 %reduce-scatter.23.cloned.1.call-start = ((), (), s32[]{:S(2)}) async-start(), calls=%async_computation.19 | async-start | bytes 17825792 | tf_op jit(solution)/shard_map/reduce_scatter | solution.py:254
  420.7 561.6 %reduce-scatter.21.cloned.1.call-start = ((), (), s32[]{:S(2)}) async-start(), calls=%async_computation.18 | async-start | bytes 17825792 | tf_op jit(solution)/shard_map/reduce_scatter | solution.py:254
  430.3 555.4 %copy-start.34 = (bf16[2,64,1024]{2,1,0:T(8,128)(2,1)S(1)}, bf16[2,64,1024]{2,1,0:T(8,128)(2,1)}, u32[]{:S(2)}) copy-start(bf16[2,64,1024]{2,1,0:T(8,128)(2,1)} %param.16) | copy-start | bytes 786436
  430.3 555.6 %copy-start.58 = (f32[1024]{0:T(1024)S(1)}, f32[1024]{0:T(1024)}, u32[]{:S(2)}) copy-start(f32[1024]{0:T(1024)} %get-tuple-element.17) | copy-start | bytes 12292
  430.3 555.6 %copy-start.59 = (f32[1024]{0:T(1024)S(1)}, f32[1024]{0:T(1024)}, u32[]{:S(2)}) copy-start(f32[1024]{0:T(1024)} %get-tuple-element.24) | copy-start | bytes 12292
  430.3 555.6 %copy-start.60 = (f32[1024]{0:T(1024)S(1)}, f32[1024]{0:T(1024)}, u32[]{:S(2)}) copy-start(f32[1024]{0:T(1024)} %get-tuple-element.61) | copy-start | bytes 12292
  430.3 555.6 %copy-start.61 = (f32[1024]{0:T(1024)S(1)}, f32[1024]{0:T(1024)}, u32[]{:S(2)}) copy-start(f32[1024]{0:T(1024)} %get-tuple-element.59) | copy-start | bytes 12292
  430.3 555.6 %copy-start.52 = (f32[4096]{0:T(1024)S(1)}, f32[4096]{0:T(1024)}, u32[]{:S(2)}) copy-start(f32[4096]{0:T(1024)} %get-tuple-element.63) | copy-start | bytes 49156
  430.3 555.6 %copy-start.53 = (f32[4096]{0:T(1024)S(1)}, f32[4096]{0:T(1024)}, u32[]{:S(2)}) copy-start(f32[4096]{0:T(1024)} %get-tuple-element.65) | copy-start | bytes 49156
  430.3 555.6 %copy-start.64 = (f32[1024]{0:T(1024)S(1)}, f32[1024]{0:T(1024)}, u32[]{:S(2)}) copy-start(f32[1024]{0:T(1024)} %get-tuple-element.28) | copy-start | bytes 12292
  430.3 555.6 %copy-start.65 = (f32[1024]{0:T(1024)S(1)}, f32[1024]{0:T(1024)}, u32[]{:S(2)}) copy-start(f32[1024]{0:T(1024)} %get-tuple-element.96) | copy-start | bytes 12292
  430.3 555.7 %copy-start.62 = (f32[1024]{0:T(1024)S(1)}, f32[1024]{0:T(1024)}, u32[]{:S(2)}) copy-start(f32[1024]{0:T(1024)} %get-tuple-element.21) | copy-start | bytes 12292
  430.4 555.7 %copy-start.63 = (f32[1024]{0:T(1024)S(1)}, f32[1024]{0:T(1024)}, u32[]{:S(2)}) copy-start(f32[1024]{0:T(1024)} %get-tuple-element.98) | copy-start | bytes 12292
  430.4 555.7 %copy-start.66 = (f32[1024]{0:T(1024)S(1)}, f32[1024]{0:T(1024)}, u32[]{:S(2)}) copy-start(f32[1024]{0:T(1024)} %get-tuple-element.69) | copy-start | bytes 12292
  430.4 555.7 %copy-start.44 = (bf16[1,64,1024]{2,1,0:T(8,128)(2,1)S(1)}, bf16[1,64,1024]{2,1,0:T(8,128)(2,1)}, u32[]{:S(2)}) copy-start(bf16[1,64,1024]{2,1,0:T(8,128)(2,1)} %get-tuple-element.84) | copy-start | bytes 393220
  430.4 555.7 %copy-start.45 = (bf16[1,64,1024]{2,1,0:T(8,128)(2,1)S(1)}, bf16[1,64,1024]{2,1,0:T(8,128)(2,1)}, u32[]{:S(2)}) copy-start(bf16[1,64,1024]{2,1,0:T(8,128)(2,1)} %get-tuple-element.85) | copy-start | bytes 393220
  430.4 556.4 %copy-start.46 = (bf16[64,1024]{1,0:T(8,128)(2,1)S(1)}, bf16[64,1024]{1,0:T(8,128)(2,1)}, u32[]{:S(2)}) copy-start(bf16[64,1024]{1,0:T(8,128)(2,1)} %reduce-scatter.11.cloned.1.call-done) | copy-start | bytes 393220
  430.4 556.4 %copy-start.47 = (bf16[64,1024]{1,0:T(8,128)(2,1)S(1)}, bf16[64,1024]{1,0:T(8,128)(2,1)}, u32[]{:S(2)}) copy-start(bf16[64,1024]{1,0:T(8,128)(2,1)} %reduce-scatter.15.cloned.1.call-done) | copy-start | bytes 393220
  430.4 626.8 %copy-start.17 = (f32[64,1024]{1,0:T(8,128)S(1)}, f32[64,1024]{1,0:T(8,128)}, u32[]{:S(2)}) copy-start(f32[64,1024]{1,0:T(8,128)} %copy-done.16) | copy-start | bytes 786436
  430.4 626.8 %copy-start.72 = (f32[64]{0:T(128)S(1)}, f32[64]{0:T(128)}, u32[]{:S(2)}) copy-start(f32[64]{0:T(128)} %copy-done.71) | copy-start | bytes 772
  430.5 637.2 %all-reduce.23.cloned.1.call-start = ((), (), s32[]{:S(2)}) async-start(), calls=%async_computation.20 | async-start | bytes 3145728 | tf_op jit(solution)/shard_map/psum | solution.py:256
  (75 other events, 1748.1 us)
Sparse Core Ops, SparseCore 0:
  10.4 91.9 all-gather.5
  104.6 41.6 all-gather.7
  148.4 93.0 all-gather.9
  243.5 72.8 all-gather.11
  350.6 9.7 reduce-scatter.8
  362.5 11.6 reduce-scatter.10
  377.0 11.6 reduce-scatter.12
  391.6 11.6 reduce-scatter.14
  407.2 72.4 reduce-scatter.18
  484.1 133.6 reduce-scatter.16
  622.5 177.7 reduce-scatter.22
  804.8 177.5 reduce-scatter.20
  985.5 51.0 all-reduce.22
